TPU v7x, 32 devices: a whole 2x2x4 slice. The times are simulated.
32 devices in a mesh: width: 4 (over z), row: 4 (over y, core), src: 2 (over x).
Axes of the slice: x: 2, y: 2, z: 4, core: 2. Of those that a mesh axis runs over, the one named last changes fastest.
Arguments:
- query_rows: bfloat16 [1024, 8192], P('row', 'width'), may hold values from -150 to 150
- key_rows: bfloat16 [1024, 1024], P('src', 'width'), may hold values from -7 to 7
- value_rows: bfloat16 [1024, 1024], P('src'), may hold values from -6 to 6
- out_proj: bfloat16 [8192, 8192], P(('row', 'src'), 'width'), may hold values from -0.0625 to 0.0625
Outputs:
- share: float32 [1024, 1024], P('row', ('src', 'width'))
All inputs are finite; a program needn't handle non-finite values.
Results may differ from a plain program's by a relative error of at most 0.0014.
Values may be sent and summed in bfloat16 or wider, within the bound.
No kernel may reach another device: no remote copies, remote signals or barrier semaphores. Data moves between devices by JAX's collectives and lax.ppermute only.
A program may use at most 384 MiB of HBM per device.

v0:
```python
import functools
import math

import jax
import jax.numpy as jnp
from jax import lax
from jax.experimental import pallas as pl
from jax.experimental.pallas import tpu as pltpu
from jax.sharding import PartitionSpec as P

H = 64
KV = 8
HD = 128
GROUP = H // KV
LANES = 128
FIRST = 256


def rotated(value, axis, shift):
    size = lax.axis_size(axis)
    return lax.ppermute(value, axis, [(k, (k + shift) % size) for k in range(size)])


def gathered(value, axis):
    size = lax.axis_size(axis)
    return [value] + [rotated(value, axis, shift) for shift in range(1, size)]


def in_order(entries, axis):
    size = len(entries)
    here = lax.axis_index(axis)
    stacked = jnp.stack(entries[::-1])
    return jnp.roll(stacked, here + 1, axis=0) if size > 1 else stacked


def swapped(value, axis, bit):
    size = lax.axis_size(axis)
    return lax.ppermute(value, axis, [(k, k ^ bit) for k in range(size)])


def spread(value, count, axis):
    size = lax.axis_size(axis)
    held = {0: value}
    bit = size // 2
    while bit > 1:
        held.update({k | bit: swapped(v[:count], axis, bit) for k, v in list(held.items())})
        bit //= 2
    held.update({k | 1: swapped(v, axis, 1) for k, v in list(held.items())})
    return [held[k] for k in range(size)]


def shared_halves(value):
    count = value.shape[0]
    odd = lax.axis_index("row") % 2
    half = lax.dynamic_slice_in_dim(value, odd * (count // 2), count // 2, 0)
    mine = in_order(gathered(half, "src"), "src")
    other = swapped(mine, "row", 1)
    first = jnp.where(odd == 0, mine, other)
    second = jnp.where(odd == 0, other, mine)
    return jnp.stack([first, second], axis=1).reshape((-1,) + value.shape[1:])


def after(value, earlier):
    return lax.optimization_barrier((value, earlier))[0]


def line_gather(value, axis):
    size = lax.axis_size(axis)
    here = lax.axis_index(axis)
    if size != 4:
        held = [value] + [swapped(value, axis, k) for k in range(1, size)]
        return held, [here ^ k for k in range(size)]
    inner = (here == 1) | (here == 2)
    across, outward = [(1, 2), (2, 1)], [(1, 0), (2, 3)]
    near = swapped(value, axis, 1)
    middle = lax.ppermute(value, axis, across)
    far = lax.ppermute(near, axis, across)
    second = jnp.where(inner, middle, lax.ppermute(middle, axis, outward))
    last = jnp.where(inner, far, lax.ppermute(after(far, second), axis, outward))
    origins = [
        here,
        here ^ 1,
        jnp.array([2, 2, 1, 1], jnp.int32)[here],
        jnp.array([3, 3, 0, 0], jnp.int32)[here],
    ]
    return [value, near, second, last], origins


PAD = 8
UNROLL = 32
HEADS_TOGETHER = 4
STEP = 128


def piece_starts(here_src, rows, parts, row_devices):
    piece = rows // parts
    return [
        row * rows + (here_src if row % 2 == 0 else parts - 1 - here_src) * piece
        for row in range(row_devices)
    ]


def weights_kernel(
    place_ref, *refs, rows, parts, row_devices, sources, limits, scale
):
    pieces = refs[:row_devices]
    o_ref, stage, scales, held, keys = refs[row_devices:]
    here_src, here_row = place_ref[0], place_ref[1]
    piece = rows // parts
    here_heads = held.shape[1] // HD
    key_width = keys.shape[1]
    chunk = math.gcd(rows, 256)
    packs = held.shape[1] // key_width
    pack_rows = pieces[0].shape[0] - piece
    share = sources // parts // 2
    step_at = pl.program_id(0)

    @pl.when(step_at == 0)
    def _():
        for bit, ref in enumerate(pieces[:2]):
            origin = (here_row ^ bit) % 2
            for pack in range(packs):
                src, inner = divmod(pack * pack_rows, share)
                at = src * (sources // parts) + origin * share + inner
                keys[pl.ds(pl.multiple_of(at, pack_rows), pack_rows), :] = ref[
                    piece:, pack * key_width : (pack + 1) * key_width
                ]

    per = max(1, LANES // piece)
    for slot in range(per):
        want = step_at * per + slot
        for bit, ref in enumerate(pieces):

            @pl.when(here_row ^ bit == want)
            def _(ref=ref, slot=slot):
                held[slot * piece : (slot + 1) * piece, :] = ref[:piece, :]

    def folded(value, combine):
        return combine(value.reshape(-1, 8, LANES), axis=0)

    for block, (low, high) in enumerate(limits):

        @pl.when(step_at == block)
        def _(block=block, low=low, high=high):
            local = block * LANES + lax.broadcasted_iota(jnp.int32, (1, LANES), 1)
            row = local // piece
            turn = jnp.where(row % 2 == 0, here_src, parts - 1 - here_src)
            position = row * rows + turn * piece + local % piece
            together = math.gcd(HEADS_TOGETHER, here_heads)

            def several(step, carry):
                for inner in range(together):
                    head = step * together + inner
                    group = head // GROUP
                    query = held[:, pl.ds(pl.multiple_of(head * HD, HD), HD)]
                    columns = pl.ds(pl.multiple_of(group * HD, HD), HD)
                    peak = jnp.full((8, LANES), -1e30, jnp.float32)
                    for at in range(0, high, chunk):
                        scores = lax.dot_general(
                            keys[at : at + chunk, columns],
                            query,
                            (((1,), (1,)), ((), ())),
                            preferred_element_type=jnp.float32,
                        )
                        if at >= low:
                            source = at + lax.broadcasted_iota(jnp.int32, (chunk, LANES), 0)
                            scores = jnp.where(source <= position, scores, jnp.float32(-1e30))
                        stage[head, at : at + chunk, :] = scores
                        peak = jnp.maximum(peak, folded(scores, jnp.max))
                    peak = jnp.max(peak, axis=0, keepdims=True)
                    mass = jnp.zeros((8, LANES), jnp.float32)
                    for at in range(0, high, chunk):
                        grown = jnp.exp2((stage[head, at : at + chunk, :] - peak) * scale)
                        stage[head, at : at + chunk, :] = grown
                        mass = mass + folded(grown, jnp.sum)
                    mass = jnp.sum(mass, axis=0, keepdims=True)
                    scales[pl.ds(pl.multiple_of(head * 8, 8), 8), :] = jnp.broadcast_to(
                        1.0 / mass, (8, LANES)
                    )
                return carry

            lax.fori_loop(0, here_heads // together, several, 0)
            flat = stage.reshape(here_heads * (sources + PAD), LANES)
            factors = scales[pl.ds(0, here_heads, stride=8), :]
            each = 16

            def cast(step, carry):
                for inner in range(each):
                    at = step * each + inner
                    value = flat[pl.ds(at, here_heads, stride=sources + PAD), :]
                    o_ref[at] = (value * factors).astype(jnp.bfloat16)
                return carry

            lax.fori_loop(0, high // each, cast, 0, unroll=2)


def head_weights(place, pieces, rows, parts, sources, key_width):
    width = pieces[0].shape[1]
    row_devices = len(pieces)
    here_heads = width // HD
    piece = rows // parts
    count = piece * row_devices
    blocks = count // LANES
    limits = [
        (
            block * LANES // piece * rows,
            (((block + 1) * LANES - 1) // piece + 1) * rows,
        )
        for block in range(blocks)
    ]
    kernel = functools.partial(
        weights_kernel,
        rows=rows,
        parts=parts,
        row_devices=row_devices,
        sources=sources,
        limits=limits,
        scale=math.log2(math.e) / math.sqrt(HD),
    )
    work = count * sources * here_heads
    return pl.pallas_call(
        kernel,
        out_shape=jax.ShapeDtypeStruct((blocks, sources, here_heads, LANES), jnp.bfloat16),
        grid_spec=pltpu.PrefetchScalarGridSpec(
            num_scalar_prefetch=1,
            grid=(blocks,),
            in_specs=[
                pl.BlockSpec(p.shape, lambda b, place: (0, 0), pipeline_mode=pl.Buffered(1))
                for p in pieces
            ],
            out_specs=pl.BlockSpec(
                (None, sources, here_heads, LANES), lambda b, place: (b, 0, 0, 0)
            ),
            scratch_shapes=[
                pltpu.VMEM((here_heads, sources + PAD, LANES), jnp.float32),
                pltpu.VMEM((here_heads * 8, LANES), jnp.float32),
                pltpu.VMEM((LANES, width), jnp.bfloat16),
                pltpu.VMEM((sources, key_width), jnp.bfloat16),
            ],
        ),
        compiler_params=pltpu.CompilerParams(vmem_limit_bytes=60 << 20),
        cost_estimate=pl.CostEstimate(
            flops=work * HD, transcendentals=work // 2, bytes_accessed=work * 2
        ),
        name="head_weights",
    )(place, *pieces)


def norms_kernel(place_ref, v_ref, *refs, rows, parts, row_devices, spans, first):
    here_src, here_row = place_ref[0], place_ref[1]
    wo_refs = refs[: parts * row_devices]
    w_refs = refs[parts * row_devices : parts * row_devices + spans]
    rest = refs[parts * row_devices + spans :]
    if first:
        o_ref, stage, flipped = rest
    else:
        before_ref, o_ref, stage, flipped = rest
    sources = v_ref.shape[0]
    local_rows, cols = wo_refs[0].shape
    span_heads = H // spans
    local_heads = local_rows // HD
    piece = rows // parts
    pitch = sources + PAD
    tiles = range(cols // LANES)
    blocks = w_refs[0].shape[0]
    for turn in range(parts):
        origin = lax.rem(here_src + parts - turn, parts)
        for bit in range(row_devices):
            base = ((here_row ^ bit) * parts + origin) * local_heads
            for step in range(local_heads):
                head = base + step
                group = head // GROUP
                values = v_ref[:, pl.ds(pl.multiple_of(group * HD, HD), HD)]
                part = wo_refs[bit * parts + turn][step * HD : (step + 1) * HD, :]
                made = jnp.dot(values, part, preferred_element_type=jnp.float32)
                at = pl.multiple_of(head * pitch, PAD)
                for tile in tiles:
                    stage[tile, pl.ds(at, sources), :] = made[:, tile * LANES : (tile + 1) * LANES]

    slots = [place_ref[2 + k] * (span_heads * pitch) for k in range(spans)]
    start = pl.program_id(0) * sources
    skipped = jnp.int32(0)
    for begin in piece_starts(here_src, rows, parts, row_devices):
        skipped = skipped + jnp.where(begin + piece <= start, 1, 0).astype(jnp.int32)
    begins = [row * piece // LANES * LANES for row in range(row_devices)]

    @pl.when(skipped == row_devices)
    def _():
        flipped[...] = jnp.zeros_like(flipped)

    for begin in sorted(set(begins)):
        fits = [row for row in range(row_devices) if begins[row] == begin]

        @pl.when((skipped >= fits[0]) & (skipped <= fits[-1]))
        def _(begin=begin):
            if begin:
                flipped[:, :begin] = jnp.zeros((sources, begin), jnp.float32)

            def several(step, carry):
                found = []
                for inner in range(UNROLL):
                    col = step * UNROLL + inner
                    attend = jnp.concatenate(
                        [
                            jnp.concatenate([ref[block, col] for ref in w_refs], axis=0)
                            for block in range(begin // LANES, blocks)
                        ],
                        axis=1,
                    )
                    made = jnp.concatenate(
                        [
                            jnp.concatenate(
                                [
                                    stage[
                                        tile, pl.ds(begin_at + col, span_heads, stride=pitch), :
                                    ].astype(jnp.bfloat16)
                                    for begin_at in slots
                                ],
                                axis=0,
                            )
                            for tile in tiles
                        ],
                        axis=1,
                    )
                    contrib = lax.dot_general(
                        made, attend, (((0,), (0,)), ((), ())), preferred_element_type=jnp.float32
                    )
                    found.append(jnp.sum(jnp.abs(contrib), axis=0, keepdims=True))
                    if len(found) == 8:
                        at = pl.multiple_of(step * UNROLL + inner - 7, 8)
                        flipped[pl.ds(at, 8), begin:] = jnp.concatenate(found, axis=0)
                        found = []
                return carry

            lax.fori_loop(0, sources // UNROLL, several, 0)

    found = flipped[...].T
    o_ref[...] = found if first else before_ref[...] + found


def partial_norms(place, values, projections, weights, before, rows, parts):
    row_devices = len(projections) // parts
    sources = values.shape[0]
    count = weights[0].shape[0] * LANES
    cols = projections[0].shape[-1]
    step = STEP
    kernel = functools.partial(
        norms_kernel,
        rows=rows,
        parts=parts,
        row_devices=row_devices,
        spans=len(weights),
        first=before is None,
    )
    in_specs = [pl.BlockSpec((step, values.shape[1]), lambda b, place: (b, 0))]
    in_specs += [
        pl.BlockSpec(p.shape, lambda b, place: (0, 0), pipeline_mode=pl.Buffered(1))
        for p in projections
    ]
    in_specs += [
        pl.BlockSpec((w.shape[0], step) + w.shape[2:], lambda b, place: (0, b, 0, 0))
        for w in weights
    ]
    args = [values, *projections, *weights]
    out_spec = pl.BlockSpec((count, step), lambda b, place: (0, b))
    if before is not None:
        in_specs.append(out_spec)
        args.append(before)
    return pl.pallas_call(
        kernel,
        out_shape=jax.ShapeDtypeStruct((count, sources), jnp.float32),
        grid_spec=pltpu.PrefetchScalarGridSpec(
            num_scalar_prefetch=1,
            grid=(sources // step,),
            in_specs=in_specs,
            out_specs=out_spec,
            scratch_shapes=[
                pltpu.VMEM((cols // LANES, H * (step + PAD), LANES), jnp.float32),
                pltpu.VMEM((step, count), jnp.float32),
            ],
        ),
        compiler_params=pltpu.CompilerParams(vmem_limit_bytes=60 << 20),
        cost_estimate=pl.CostEstimate(
            flops=count * sources * H * cols + 2 * sources * H * HD * cols,
            transcendentals=0,
            bytes_accessed=count * sources * H * 2,
        ),
        name="partial_norms",
    )(place, *args)


def whole(query_rows, key_rows, value_rows, out_proj):
    row_devices = lax.axis_size("row")
    parts = lax.axis_size("src")
    spans = lax.axis_size("width")
    here_row = lax.axis_index("row")
    here_src = lax.axis_index("src")
    here_width = lax.axis_index("width")
    rows, width = query_rows.shape
    col_count, key_width = key_rows.shape
    sources = col_count * parts
    piece = rows // parts

    share = col_count // 2
    key_part = lax.dynamic_slice_in_dim(key_rows, here_row % 2 * share, share, 0)
    key_part = in_order(gathered(key_part, "src"), "src").reshape(-1, key_width)
    packs = width // key_width
    key_part = key_part.reshape(packs, -1, key_width).transpose(1, 0, 2).reshape(-1, width)
    turn = jnp.where(here_row % 2 == 0, here_src, parts - 1 - here_src)
    mine = lax.dynamic_slice_in_dim(query_rows, turn * piece, piece, 0)
    message = jnp.concatenate([mine, key_part], axis=0)
    messages, origins = line_gather(message, "width")
    place = jnp.stack([here_src, here_row, *origins]).astype(jnp.int32)
    weights = []
    for m in messages:
        pieces = spread(m, piece, "row")
        weights.append(head_weights(place, pieces, rows, parts, sources, key_width))
    values = shared_halves(value_rows)

    _, cols = out_proj.shape
    each = cols // row_devices
    sizes = [FIRST, each - FIRST] if each > FIRST and each % LANES == 0 else [each]
    norms = None
    begin = 0
    for size in sizes:
        projections = []
        for bit in range(row_devices):
            at = (here_row ^ bit) * each + begin
            block = lax.dynamic_slice_in_dim(out_proj, at, size, 1)
            if bit:
                block = swapped(block, "row", bit)
            projections += gathered(block, "src")
        norms = partial_norms(place, values, projections, weights, norms, rows, parts)
        begin += size

    stacked = norms.reshape(row_devices, piece, sources)
    held = [
        lax.dynamic_index_in_dim(stacked, here_row ^ bit, 0, keepdims=False)
        for bit in range(row_devices)
    ]
    bit = 1
    while bit < row_devices:
        kept = [held[k] for k in range(0, len(held), 2)]
        sent = [held[k] for k in range(1, len(held), 2)]
        held = [k + swapped(v, "row", bit) for k, v in zip(kept, sent)]
        bit *= 2
    table = held[0]
    total = jnp.pad(jnp.sum(table, axis=1), (0, sources // parts - piece))[None]
    blocks = table.reshape(piece, parts, sources // parts)
    gotten = []
    for shift in range(parts):
        block = lax.dynamic_index_in_dim(blocks, (here_src + shift) % parts, 1, keepdims=False)
        block = jnp.concatenate([block, total], axis=0)
        gotten.append(rotated(block, "src", shift) if shift else block)
    gotten = in_order(gotten, "src")
    gotten = jnp.where(here_row % 2 == 0, gotten, gotten[::-1])
    total = gotten[:, piece, :piece].reshape(rows)
    table = gotten[:, :piece].reshape(rows, -1)
    last = table.shape[1] // spans
    total = total.reshape(-1, last)
    blocks = table.reshape(rows, spans, last)
    summed = None
    for shift in range(spans):
        block = lax.dynamic_index_in_dim(blocks, (here_width + shift) % spans, 1, keepdims=False)
        block = jnp.concatenate([block, total], axis=0)
        block = rotated(block, "width", shift) if shift else block
        summed = block if summed is None else summed + block
    totals = summed[rows:].reshape(rows)
    position = (here_row * rows + jnp.arange(rows, dtype=jnp.int32) + 1).astype(jnp.float32)
    return position[:, None] * summed[:rows] / totals[:, None]


def solution(mesh):
    placed = (P("row", "width"), P("src", "width"), P("src", None), P(("row", "src"), "width"))
    return jax.shard_map(
        whole, mesh=mesh, in_specs=placed, out_specs=P("row", ("src", "width")), check_vma=False
    )
```

profile of v0, /device:TPU:0, one launch (start us, length us, event | category | flops | bytes accessed | tf_op | source)
XLA Modules:
  0.0 366.8 jit_solution(5310090746893994626)
XLA Ops:
  1.0 3.0 collective-permute-start.9
  4.0 1.9 constant_dynamic-slice_fusion.15
  10.4 3.8 %collective-permute-start.13 = (bf16[192,2048]{1,0:T(8,128)(2,1)S(1)}, bf16[192,2048]{1,0:T(8,128)(2,1)S(1)}, u32[]{:S(2)}, u32[]{:S(2)}) collective-permute-start(bf16[192,2048]{1,0:T(8,128)(2,1)S(1)} %pad_maximum_fusion.1.refs_0_), channel_id=1, source_target_pairs={{0,8},{8,0},{16,24},{24,16},{1,9},{9,1},{17,25},{25,17},{2,10},{10... | collective-permute-start | bytes 2359304 | tf_op jit(solution)/shard_map/ppermute | solution.py:38
  15.5 15.1 %collective-permute-done.13.refs_0_ = bf16[192,2048]{1,0:T(8,128)(2,1)S(1)} collective-permute-done((bf16[192,2048]{1,0:T(8,128)(2,1)S(1)}, bf16[192,2048]{1,0:T(8,128)(2,1)S(1)}, u32[]{:S(2)}, u32[]{:S(2)}) %collective-permute-start.13) | collective-permute-done | bytes 786464 | tf_op jit(solution)/shard_map/ppermute | solution.py:38
  36.1 4.2 %constant_dynamic-slice_fusion.10 = (bf16[1024,256]{1,0:T(8,128)(2,1)}, bf16[1024,256]{1,0:T(8,128)(2,1)}, bf16[1024,256]{1,0:T(8,128)(2,1)}, bf16[1024,256]{1,0...) fusion(bf16[1024,2048]{1,0:T(8,128)(2,1)} %param.9, ...), kind=kLoop, calls=%fused_computation.53 | loop fusion | bytes 8388640 | tf_op jit(solution)/shard_map/dynamic_slice | solution.py:429
  40.4 8.1 %collective-permute-done.18 = bf16[192,2048]{1,0:T(8,128)(2,1)} collective-permute-done((bf16[192,2048]{1,0:T(8,128)(2,1)}, bf16[192,2048]{1,0:T(8,128)(2,1)}, u32[]{:S(2)}, u32[]{:S(2)}) %collective-permute-start.18) | collective-permute-done | bytes 786464 | tf_op jit(solution)/shard_map/ppermute | solution.py:78
  53.3 1.6 collective-permute-start.27
  54.9 8.7 %collective-permute-done.30.refs_4_ = bf16[1024,256]{1,0:T(8,128)(2,1)S(1)} collective-permute-done((bf16[1024,256]{1,0:T(8,128)(2,1)}, bf16[1024,256]{1,0:T(8,128)(2,1)S(1)}, u32[]{:S(2)}, u32[]{:S(2)}) %collective-permute-start.30) | collective-permute-done | bytes 524320 | tf_op jit(solution)/shard_map/ppermute | solution.py:38
  64.3 1.8 fusion.2
  66.1 4.4 %collective-permute-done.32.refs_6_ = bf16[1024,256]{1,0:T(8,128)(2,1)S(1)} collective-permute-done((bf16[1024,256]{1,0:T(8,128)(2,1)}, bf16[1024,256]{1,0:T(8,128)(2,1)S(1)}, u32[]{:S(2)}, u32[]{:S(2)}) %collective-permute-start.32) | collective-permute-done | bytes 524320 | tf_op jit(solution)/shard_map/ppermute | solution.py:38
  71.7 1.6 collective-permute-start.15
  73.4 1.7 collective-permute-done.23
  75.9 1.6 collective-permute-start.25
  77.5 9.2 %collective-permute-done.15.refs_2_ = bf16[128,2048]{1,0:T(8,128)(2,1)} collective-permute-done((bf16[128,2048]{1,0:T(8,128)(2,1)S(1)}, bf16[128,2048]{1,0:T(8,128)(2,1)}, u32[]{:S(2)}, u32[]{:S(2)}) %collective-permute-start.15) | collective-permute-done | bytes 524320 | tf_op jit(solution)/shard_map/ppermute | solution.py:38
  88.1 9.8 %collective-permute-done.20.refs_2_ = bf16[128,2048]{1,0:T(8,128)(2,1)} collective-permute-done((bf16[128,2048]{1,0:T(8,128)(2,1)S(1)}, bf16[128,2048]{1,0:T(8,128)(2,1)}, u32[]{:S(2)}, u32[]{:S(2)}) %collective-permute-start.20) | collective-permute-done | bytes 524320 | tf_op jit(solution)/shard_map/ppermute | solution.py:38
  97.9 10.7 %collective-permute-done.25.refs_2_ = bf16[128,2048]{1,0:T(8,128)(2,1)} collective-permute-done((bf16[128,2048]{1,0:T(8,128)(2,1)S(1)}, bf16[128,2048]{1,0:T(8,128)(2,1)}, u32[]{:S(2)}, u32[]{:S(2)}) %collective-permute-start.25) | collective-permute-done | bytes 524320 | tf_op jit(solution)/shard_map/ppermute | solution.py:38
  109.9 1.9 stack.49.place_ref
  111.8 17.4 %head_weights.4.refs_8_ = bf16[4,1024,16,128]{3,2,1,0:T(8,128)(2,1)} custom-call(s32[6]{0:T(128)} %stack.49.place_ref, bf16[192,2048]{1,0:T(8,128)(2,1)} %copy-done.4, bf16[192,2048]{1,0:T(8,128)(2,1)} %copy-done.11, bf16[128,2048]{1,0:T(8,128)(2,1)} %collective-permute-done.11.refs_2_, bf16[128,2048]{1,0:T(8,128)(2,1)} %copy-done.23), custom_call_target="tpu_custom_call" | custom-call | flops 1073741824 | bytes 16777216 | tf_op jit(solution)/shard_map/head_weights/pallas_call | solution.py:221
  129.2 1.6 collective-permute-start.5
  134.7 2.0 select_bitcast_fusion.1
  138.4 17.1 %head_weights.5.refs_9_ = bf16[4,1024,16,128]{3,2,1,0:T(8,128)(2,1)} custom-call(s32[6]{0:T(128)} %stack.49.place_ref, bf16[192,2048]{1,0:T(8,128)(2,1)} %copy-done.5, bf16[192,2048]{1,0:T(8,128)(2,1)} %copy-done.12, bf16[128,2048]{1,0:T(8,128)(2,1)} %collective-permute-done.15.refs_2_, bf16[128,2048]{1,0:T(8,128)(2,1)} %collective-permute-done.16.refs_3_), custom_call_target="tpu_custom_call" | custom-call | flops 1073741824 | bytes 16777216 | tf_op jit(solution)/shard_map/head_weights/pallas_call | solution.py:221
  155.5 17.1 %head_weights.6.refs_10_ = bf16[4,1024,16,128]{3,2,1,0:T(8,128)(2,1)} custom-call(s32[6]{0:T(128)} %stack.49.place_ref, bf16[192,2048]{1,0:T(8,128)(2,1)} %copy-done.2, bf16[192,2048]{1,0:T(8,128)(2,1)} %collective-permute-done.19.refs_1_, bf16[128,2048]{1,0:T(8,128)(2,1)} %collective-permute-done.20.refs_2_, bf16[128,2048]{1,0:T(8,128)(2,1)} %collective-permute-done.21.refs_3_), custom_call_target="tpu_custom_call" | custom-call | flops 1073741824 | bytes 16777216 | tf_op jit(solution)/shard_map/head_weights/pallas_call | solution.py:221
  172.7 17.3 %head_weights.7.refs_11_ = bf16[4,1024,16,128]{3,2,1,0:T(8,128)(2,1)} custom-call(s32[6]{0:T(128)} %stack.49.place_ref, bf16[192,2048]{1,0:T(8,128)(2,1)} %copy-done.3, bf16[192,2048]{1,0:T(8,128)(2,1)} %collective-permute-done.24.refs_1_, bf16[128,2048]{1,0:T(8,128)(2,1)} %collective-permute-done.25.refs_2_, bf16[128,2048]{1,0:T(8,128)(2,1)} %collective-permute-done.26.refs_3_), custom_call_target="tpu_custom_call" | custom-call | flops 1073741824 | bytes 16777216 | tf_op jit(solution)/shard_map/head_weights/pallas_call | solution.py:221
  194.1 64.7 %partial_norms.2.refs_12_ = f32[512,1024]{1,0:T(8,128)} custom-call(s32[6]{0:T(128)} %stack.49.place_ref, bf16[1024,1024]{1,0:T(8,128)(2,1)} %bitcast.44, bf16[1024,256]{1,0:T(8,128)(2,1)} %get-tuple-element.11.refs_0_, bf16[1024,256]{1,0:T(8,128)(2,1)} %copy-done.17, bf16[1024,256]{1,0:T(8,128)(2,1)} %collective-permute-done.28.refs_2_, ...), custom_call_target="tpu_custom_call" | custom-call | flops 12884901888 | bytes 67108864 | tf_op jit(solution)/shard_map/partial_norms/pallas_call | solution.py:369
  260.9 65.0 %partial_norms.3 = f32[512,1024]{1,0:T(8,128)} custom-call(s32[6]{0:T(128)} %stack.49.place_ref, bf16[1024,1024]{1,0:T(8,128)(2,1)} %bitcast.45, bf16[1024,256]{1,0:T(8,128)(2,1)} %get-tuple-element.15.refs_0_, bf16[1024,256]{1,0:T(8,128)(2,1)} %copy-done.19, bf16[1024,256]{1,0:T(8,128)(2,1)} %copy-done.15, bf16[1024,256]{1,0:T(8,128)(2,1)} %copy-done.20, ...), custom_call_target="tpu_custom_call" | custom-call | flops 12884901888 | bytes 67108864 | tf_op jit(solution)/shard_map/partial_norms/pallas_call | solution.py:369
  325.9 1.7 constant_dynamic-slice_fusion.9
  330.8 1.6 collective-permute-start.36
  332.6 12.3 %collective-permute-done.36 = f32[128,1024]{0,1:T(8,128)S(1)} collective-permute-done((f32[128,1024]{0,1:T(8,128)S(1)}, f32[128,1024]{0,1:T(8,128)S(1)}, u32[]{:S(2)}, u32[]{:S(2)}) %collective-permute-start.36) | collective-permute-done | bytes 524320 | tf_op jit(solution)/shard_map/ppermute | solution.py:38
  345.5 7.8 %collective-permute-done.37 = f32[129,512]{1,0:T(8,128)S(1)} collective-permute-done((f32[129,512]{1,0:T(8,128)S(1)}, f32[129,512]{1,0:T(8,128)S(1)}, u32[]{:S(2)}, u32[]{:S(2)}) %collective-permute-start.37) | collective-permute-done | bytes 264224 | tf_op jit(solution)/shard_map/ppermute | solution.py:21
  354.3 3.0 collective-permute-start.39
  358.2 4.4 %collective-permute-done.38 = f32[258,128]{1,0:T(8,128)S(1)} collective-permute-done((f32[258,128]{1,0:T(8,128)S(1)}, f32[258,128]{1,0:T(8,128)S(1)}, u32[]{:S(2)}, u32[]{:S(2)}) %collective-permute-start.38) | collective-permute-done | bytes 132128 | tf_op jit(solution)/shard_map/ppermute | solution.py:21
  362.6 3.3 collective-permute-done.39
  (154 shorter events, 40.7 us)
Async XLA Ops:
  10.4 20.2 %collective-permute-start.13 = (bf16[192,2048]{1,0:T(8,128)(2,1)S(1)}, bf16[192,2048]{1,0:T(8,128)(2,1)S(1)}, u32[]{:S(2)}, u32[]{:S(2)}) collective-permute-start(bf16[192,2048]{1,0:T(8,128)(2,1)S(1)} %pad_maximum_fusion.1.refs_0_), channel_id=1, source_target_pairs={{0,8},{8,0},{16,24},{24,16},{1,9},{9,1},{17,25},{25,17},{2,10},{10... | collective-permute-start | bytes 2359304 | tf_op jit(solution)/shard_map/ppermute | solution.py:38
  14.3 34.3 %collective-permute-start.18 = (bf16[192,2048]{1,0:T(8,128)(2,1)}, bf16[192,2048]{1,0:T(8,128)(2,1)}, u32[]{:S(2)}, u32[]{:S(2)}) collective-permute-start(bf16[192,2048]{1,0:T(8,128)(2,1)} %collective-permute-done.17), channel_id=1, source_target_pairs={{8,0},{16,24},{9,1},{17,25},{10,2},{18,26},{11,3},{19,27},{12,4},{... | collective-permute-start | bytes 2359304 | tf_op jit(solution)/shard_map/ppermute | solution.py:78
  30.7 19.4 %collective-permute-start.22 = (bf16[192,2048]{1,0:T(8,128)(2,1)S(1)}, bf16[192,2048]{1,0:T(8,128)(2,1)}, u32[]{:S(2)}, u32[]{:S(2)}) collective-permute-start(bf16[192,2048]{1,0:T(8,128)(2,1)S(1)} %collective-permute-done.13.refs_0_), channel_id=1, source_target_pairs={{8,16},{16,8},{9,17},{17,9},{10,18},{18,10},{11,19},{19,11},{12,20... | collective-permute-start | bytes 2359304 | tf_op jit(solution)/shard_map/ppermute | solution.py:77
  32.2 19.1 %collective-permute-start.11 = (bf16[128,2048]{1,0:T(8,128)(2,1)}, bf16[128,2048]{1,0:T(8,128)(2,1)}, u32[]{:S(2)}, u32[]{:S(2)}) collective-permute-start(bf16[128,2048]{1,0:T(8,128)(2,1)} %constant_dynamic-slice_fusion.15), channel_id=1, source_target_pairs={{0,4},{2,6},{4,0},{6,2},{1,5},{3,7},{5,1},{7,3},{8,12},{10,14},{12... | collective-permute-start | bytes 1572872 | tf_op jit(solution)/shard_map/ppermute | solution.py:38
  34.6 17.4 %collective-permute-start = (bf16[256,1024]{1,0:T(8,128)(2,1)}, bf16[256,1024]{1,0:T(8,128)(2,1)S(1)}, u32[]{:S(2)}, u32[]{:S(2)}) collective-permute-start(bf16[256,1024]{1,0:T(8,128)(2,1)} %constant_dynamic-slice_fusion.20), channel_id=1, source_target_pairs={{0,1},{1,0},{2,3},{3,2},{4,5},{5,4},{6,7},{7,6},{8,9},{9,8},{10,11... | collective-permute-start | bytes 1572872 | tf_op jit(solution)/shard_map/ppermute | solution.py:21
  40.4 12.9 %collective-permute-start.28 = (bf16[1024,256]{1,0:T(8,128)(2,1)}, bf16[1024,256]{1,0:T(8,128)(2,1)}, u32[]{:S(2)}, u32[]{:S(2)}) collective-permute-start(bf16[1024,256]{1,0:T(8,128)(2,1)} %get-tuple-element.10), channel_id=1, source_target_pairs={{0,2},{2,0},{4,6},{6,4},{1,3},{3,1},{5,7},{7,5},{8,10},{10,8},{12,... | collective-permute-start | bytes 1572872 | tf_op jit(solution)/shard_map/ppermute | solution.py:38
  48.5 15.0 %collective-permute-start.30 = (bf16[1024,256]{1,0:T(8,128)(2,1)}, bf16[1024,256]{1,0:T(8,128)(2,1)S(1)}, u32[]{:S(2)}, u32[]{:S(2)}) collective-permute-start(bf16[1024,256]{1,0:T(8,128)(2,1)} %get-tuple-element.16), channel_id=1, source_target_pairs={{0,4},{2,6},{4,0},{6,2},{1,5},{3,7},{5,1},{7,3},{8,12},{10,14},{12... | collective-permute-start | bytes 1572872 | tf_op jit(solution)/shard_map/ppermute | solution.py:38
  50.1 20.4 %collective-permute-start.32 = (bf16[1024,256]{1,0:T(8,128)(2,1)}, bf16[1024,256]{1,0:T(8,128)(2,1)S(1)}, u32[]{:S(2)}, u32[]{:S(2)}) collective-permute-start(bf16[1024,256]{1,0:T(8,128)(2,1)} %get-tuple-element.9), channel_id=1, source_target_pairs={{0,6},{2,4},{4,2},{6,0},{1,7},{3,5},{5,3},{7,1},{8,14},{10,12},{12... | collective-permute-start | bytes 1572872 | tf_op jit(solution)/shard_map/ppermute | solution.py:38
  51.3 22.0 %collective-permute-start.10 = (bf16[192,2048]{1,0:T(8,128)(2,1)S(1)}, bf16[192,2048]{1,0:T(8,128)(2,1)S(1)}, u32[]{:S(2)}, u32[]{:S(2)}) collective-permute-start(bf16[192,2048]{1,0:T(8,128)(2,1)S(1)} %pad_maximum_fusion.1.refs_0_), channel_id=1, source_target_pairs={{0,2},{2,0},{4,6},{6,4},{1,3},{3,1},{5,7},{7,5},{8,10},{10,8},{12,... | collective-permute-start | bytes 2359304 | tf_op jit(solution)/shard_map/ppermute | solution.py:38
  52.0 23.2 %collective-permute-start.23 = (bf16[192,2048]{1,0:T(8,128)(2,1)}, bf16[192,2048]{1,0:T(8,128)(2,1)S(1)}, u32[]{:S(2)}, u32[]{:S(2)}) collective-permute-start(bf16[192,2048]{1,0:T(8,128)(2,1)} %collective-permute-done.22), channel_id=1, source_target_pairs={{8,0},{16,24},{9,1},{17,25},{10,2},{18,26},{11,3},{19,27},{12,4},{... | collective-permute-start | bytes 2359304 | tf_op jit(solution)/shard_map/ppermute | solution.py:79
  53.3 18.2 %collective-permute-start.27 = (bf16[1024,256]{1,0:T(8,128)(2,1)}, bf16[1024,256]{1,0:T(8,128)(2,1)S(1)}, u32[]{:S(2)}, u32[]{:S(2)}) collective-permute-start(bf16[1024,256]{1,0:T(8,128)(2,1)} %get-tuple-element.11.refs_0_), channel_id=1, source_target_pairs={{0,1},{1,0},{2,3},{3,2},{4,5},{5,4},{6,7},{7,6},{8,9},{9,8},{10,11... | collective-permute-start | bytes 1572872 | tf_op jit(solution)/shard_map/ppermute | solution.py:21
  70.5 16.2 %collective-permute-start.1 = (bf16[2,256,1024]{2,1,0:T(8,128)(2,1)S(1)}, bf16[2,256,1024]{2,1,0:T(8,128)(2,1)S(1)}, u32[]{:S(2)}, u32[]{:S(2)}) collective-permute-start(bf16[2,256,1024]{2,1,0:T(8,128)(2,1)S(1)} %fusion.2), channel_id=1, source_target_pairs={{0,2},{2,0},{4,6},{6,4},{1,3},{3,1},{5,7},{7,5},{8,10},{10,8},{12,... | collective-permute-start | bytes 3145736 | tf_op jit(solution)/shard_map/ppermute | solution.py:38
  71.7 15.0 %collective-permute-start.15 = (bf16[128,2048]{1,0:T(8,128)(2,1)S(1)}, bf16[128,2048]{1,0:T(8,128)(2,1)}, u32[]{:S(2)}, u32[]{:S(2)}) collective-permute-start(bf16[128,2048]{1,0:T(8,128)(2,1)S(1)} %slice.28), channel_id=1, source_target_pairs={{0,4},{2,6},{4,0},{6,2},{1,5},{3,7},{5,1},{7,3},{8,12},{10,14},{12... | collective-permute-start | bytes 1572872 | tf_op jit(solution)/shard_map/ppermute | solution.py:38
  73.3 13.9 %collective-permute-start.14 = (bf16[192,2048]{1,0:T(8,128)(2,1)S(1)}, bf16[192,2048]{1,0:T(8,128)(2,1)S(1)}, u32[]{:S(2)}, u32[]{:S(2)}) collective-permute-start(bf16[192,2048]{1,0:T(8,128)(2,1)S(1)} %copy-done.6), channel_id=1, source_target_pairs={{0,2},{2,0},{4,6},{6,4},{1,3},{3,1},{5,7},{7,5},{8,10},{10,8},{12,... | collective-permute-start | bytes 2359304 | tf_op jit(solution)/shard_map/ppermute | solution.py:38
  75.2 22.7 %collective-permute-start.20 = (bf16[128,2048]{1,0:T(8,128)(2,1)S(1)}, bf16[128,2048]{1,0:T(8,128)(2,1)}, u32[]{:S(2)}, u32[]{:S(2)}) collective-permute-start(bf16[128,2048]{1,0:T(8,128)(2,1)S(1)} %slice.29), channel_id=1, source_target_pairs={{0,4},{2,6},{4,0},{6,2},{1,5},{3,7},{5,1},{7,3},{8,12},{10,14},{12... | collective-permute-start | bytes 1572872 | tf_op jit(solution)/shard_map/ppermute | solution.py:38
  75.9 32.7 %collective-permute-start.25 = (bf16[128,2048]{1,0:T(8,128)(2,1)S(1)}, bf16[128,2048]{1,0:T(8,128)(2,1)}, u32[]{:S(2)}, u32[]{:S(2)}) collective-permute-start(bf16[128,2048]{1,0:T(8,128)(2,1)S(1)} %slice.30), channel_id=1, source_target_pairs={{0,4},{2,6},{4,0},{6,2},{1,5},{3,7},{5,1},{7,3},{8,12},{10,14},{12... | collective-permute-start | bytes 1572872 | tf_op jit(solution)/shard_map/ppermute | solution.py:38
  86.7 44.1 %collective-permute-start.19 = (bf16[192,2048]{1,0:T(8,128)(2,1)S(1)}, bf16[192,2048]{1,0:T(8,128)(2,1)}, u32[]{:S(2)}, u32[]{:S(2)}) collective-permute-start(bf16[192,2048]{1,0:T(8,128)(2,1)S(1)} %broadcast_select_fusion.1.refs_0_), channel_id=1, source_target_pairs={{0,2},{2,0},{4,6},{6,4},{1,3},{3,1},{5,7},{7,5},{8,10},{10,8},{12,... | collective-permute-start | bytes 2359304 | tf_op jit(solution)/shard_map/ppermute | solution.py:38
  86.7 45.9 %collective-permute-start.24 = (bf16[192,2048]{1,0:T(8,128)(2,1)S(1)}, bf16[192,2048]{1,0:T(8,128)(2,1)}, u32[]{:S(2)}, u32[]{:S(2)}) collective-permute-start(bf16[192,2048]{1,0:T(8,128)(2,1)S(1)} %broadcast_select_fusion.refs_0_), channel_id=1, source_target_pairs={{0,2},{2,0},{4,6},{6,4},{1,3},{3,1},{5,7},{7,5},{8,10},{10,8},{12,... | collective-permute-start | bytes 2359304 | tf_op jit(solution)/shard_map/ppermute | solution.py:38
  87.2 42.0 %collective-permute-start.16 = (bf16[128,2048]{1,0:T(8,128)(2,1)}, bf16[128,2048]{1,0:T(8,128)(2,1)}, u32[]{:S(2)}, u32[]{:S(2)}) collective-permute-start(bf16[128,2048]{1,0:T(8,128)(2,1)} %collective-permute-done.15.refs_2_), channel_id=1, source_target_pairs={{0,2},{2,0},{4,6},{6,4},{1,3},{3,1},{5,7},{7,5},{8,10},{10,8},{12,... | collective-permute-start | bytes 1572872 | tf_op jit(solution)/shard_map/ppermute | solution.py:38
  97.9 33.2 %collective-permute-start.21 = (bf16[128,2048]{1,0:T(8,128)(2,1)}, bf16[128,2048]{1,0:T(8,128)(2,1)}, u32[]{:S(2)}, u32[]{:S(2)}) collective-permute-start(bf16[128,2048]{1,0:T(8,128)(2,1)} %collective-permute-done.20.refs_2_), channel_id=1, source_target_pairs={{0,2},{2,0},{4,6},{6,4},{1,3},{3,1},{5,7},{7,5},{8,10},{10,8},{12,... | collective-permute-start | bytes 1572872 | tf_op jit(solution)/shard_map/ppermute | solution.py:38
  108.6 24.6 %collective-permute-start.26 = (bf16[128,2048]{1,0:T(8,128)(2,1)}, bf16[128,2048]{1,0:T(8,128)(2,1)}, u32[]{:S(2)}, u32[]{:S(2)}) collective-permute-start(bf16[128,2048]{1,0:T(8,128)(2,1)} %collective-permute-done.25.refs_2_), channel_id=1, source_target_pairs={{0,2},{2,0},{4,6},{6,4},{1,3},{3,1},{5,7},{7,5},{8,10},{10,8},{12,... | collective-permute-start | bytes 1572872 | tf_op jit(solution)/shard_map/ppermute | solution.py:38
  129.2 60.7 %collective-permute-start.5 = (bf16[1024,256]{1,0:T(8,128)(2,1)}, bf16[1024,256]{1,0:T(8,128)(2,1)}, u32[]{:S(2)}, u32[]{:S(2)}) collective-permute-start(bf16[1024,256]{1,0:T(8,128)(2,1)} %get-tuple-element.13), channel_id=1, source_target_pairs={{0,4},{2,6},{4,0},{6,2},{1,5},{3,7},{5,1},{7,3},{8,12},{10,14},{12... | collective-permute-start | bytes 1572872 | tf_op jit(solution)/shard_map/ppermute | solution.py:38
  130.8 59.7 %collective-permute-start.7 = (bf16[1024,256]{1,0:T(8,128)(2,1)}, bf16[1024,256]{1,0:T(8,128)(2,1)S(1)}, u32[]{:S(2)}, u32[]{:S(2)}) collective-permute-start(bf16[1024,256]{1,0:T(8,128)(2,1)} %get-tuple-element.12), channel_id=1, source_target_pairs={{0,6},{2,4},{4,2},{6,0},{1,7},{3,5},{5,3},{7,1},{8,14},{10,12},{12... | collective-permute-start | bytes 1572872 | tf_op jit(solution)/shard_map/ppermute | solution.py:38
  131.1 61.0 %collective-permute-start.29 = (bf16[1024,256]{1,0:T(8,128)(2,1)}, bf16[1024,256]{1,0:T(8,128)(2,1)}, u32[]{:S(2)}, u32[]{:S(2)}) collective-permute-start(bf16[1024,256]{1,0:T(8,128)(2,1)} %collective-permute-done.28.refs_2_), channel_id=1, source_target_pairs={{0,1},{1,0},{2,3},{3,2},{4,5},{5,4},{6,7},{7,6},{8,9},{9,8},{10,11... | collective-permute-start | bytes 1572872 | tf_op jit(solution)/shard_map/ppermute | solution.py:21
  132.6 60.0 %collective-permute-start.31 = (bf16[1024,256]{1,0:T(8,128)(2,1)}, bf16[1024,256]{1,0:T(8,128)(2,1)}, u32[]{:S(2)}, u32[]{:S(2)}) collective-permute-start(bf16[1024,256]{1,0:T(8,128)(2,1)} %copy-done.13), channel_id=1, source_target_pairs={{0,1},{1,0},{2,3},{3,2},{4,5},{5,4},{6,7},{7,6},{8,9},{9,8},{10,11... | collective-permute-start | bytes 1572872 | tf_op jit(solution)/shard_map/ppermute | solution.py:21
  133.2 61.0 %collective-permute-start.33 = (bf16[1024,256]{1,0:T(8,128)(2,1)}, bf16[1024,256]{1,0:T(8,128)(2,1)}, u32[]{:S(2)}, u32[]{:S(2)}) collective-permute-start(bf16[1024,256]{1,0:T(8,128)(2,1)} %copy-done.14), channel_id=1, source_target_pairs={{0,1},{1,0},{2,3},{3,2},{4,5},{5,4},{6,7},{7,6},{8,9},{9,8},{10,11... | collective-permute-start | bytes 1572872 | tf_op jit(solution)/shard_map/ppermute | solution.py:21
  190.0 68.9 %collective-permute-start.2 = (bf16[1024,256]{1,0:T(8,128)(2,1)S(1)}, bf16[1024,256]{1,0:T(8,128)(2,1)S(1)}, u32[]{:S(2)}, u32[]{:S(2)}) collective-permute-start(bf16[1024,256]{1,0:T(8,128)(2,1)S(1)} %copy-done.7), channel_id=1, source_target_pairs={{0,1},{1,0},{2,3},{3,2},{4,5},{5,4},{6,7},{7,6},{8,9},{9,8},{10,11... | collective-permute-start | bytes 1572872 | tf_op jit(solution)/shard_map/ppermute | solution.py:21
  190.6 68.3 %collective-permute-start.4 = (bf16[1024,256]{1,0:T(8,128)(2,1)S(1)}, bf16[1024,256]{1,0:T(8,128)(2,1)S(1)}, u32[]{:S(2)}, u32[]{:S(2)}) collective-permute-start(bf16[1024,256]{1,0:T(8,128)(2,1)S(1)} %copy-done.16), channel_id=1, source_target_pairs={{0,1},{1,0},{2,3},{3,2},{4,5},{5,4},{6,7},{7,6},{8,9},{9,8},{10,11... | collective-permute-start | bytes 1572872 | tf_op jit(solution)/shard_map/ppermute | solution.py:21
  192.1 66.8 %collective-permute-start.6 = (bf16[1024,256]{1,0:T(8,128)(2,1)}, bf16[1024,256]{1,0:T(8,128)(2,1)S(1)}, u32[]{:S(2)}, u32[]{:S(2)}) collective-permute-start(bf16[1024,256]{1,0:T(8,128)(2,1)} %collective-permute-done.5.refs_4_), channel_id=1, source_target_pairs={{0,1},{1,0},{2,3},{3,2},{4,5},{5,4},{6,7},{7,6},{8,9},{9,8},{10,11... | collective-permute-start | bytes 1572872 | tf_op jit(solution)/shard_map/ppermute | solution.py:21
  192.7 66.3 %collective-permute-start.8 = (bf16[1024,256]{1,0:T(8,128)(2,1)S(1)}, bf16[1024,256]{1,0:T(8,128)(2,1)S(1)}, u32[]{:S(2)}, u32[]{:S(2)}) collective-permute-start(bf16[1024,256]{1,0:T(8,128)(2,1)S(1)} %collective-permute-done.7.refs_6_), channel_id=1, source_target_pairs={{0,1},{1,0},{2,3},{3,2},{4,5},{5,4},{6,7},{7,6},{8,9},{9,8},{10,11... | collective-permute-start | bytes 1572872 | tf_op jit(solution)/shard_map/ppermute | solution.py:21
  330.8 14.0 %collective-permute-start.36 = (f32[128,1024]{0,1:T(8,128)S(1)}, f32[128,1024]{0,1:T(8,128)S(1)}, u32[]{:S(2)}, u32[]{:S(2)}) collective-permute-start(f32[128,1024]{0,1:T(8,128)S(1)} %bitcast_add_fusion), channel_id=1, source_target_pairs={{0,4},{2,6},{4,0},{6,2},{1,5},{3,7},{5,1},{7,3},{8,12},{10,14},{12... | collective-permute-start | bytes 1572872 | tf_op jit(solution)/shard_map/ppermute | solution.py:38
  354.3 11.6 %collective-permute-start.39 = (f32[258,128]{1,0:T(8,128)S(1)}, f32[258,128]{1,0:T(8,128)S(1)}, u32[]{:S(2)}, u32[]{:S(2)}) collective-permute-start(f32[258,128]{1,0:T(8,128)S(1)} %get-tuple-element.32), channel_id=1, source_target_pairs={{0,16},{8,24},{16,0},{24,8},{1,17},{9,25},{17,1},{25,9},{2,18},{10... | collective-permute-start | bytes 396296 | tf_op jit(solution)/shard_map/ppermute | solution.py:21
  (36 other events, 618.7 us)
where the time goes:
time: 368 us; the launch traced here: 367 us
  Pallas kernels  199 us (54%)
  waiting for transfers between devices  97.4 us (26%)
  starting transfers between devices  40.7 us (11%)
  local copies, waits for them, and re-layouts  21.5 us (6%)
  other arithmetic  7.9 us (2%)
    pallas_call x2, Pallas kernels, partial_norms(): pl.pallas_call(kernel, out_shape=jax.ShapeDtypeStruct((count, sources), j...  130 us
    ppermute x23, waiting for transfers between devices, swapped(): return lax.ppermute(value, axis, [(k, k ^ bit) for k in range(size)])  71.3 us
    pallas_call x4, Pallas kernels, head_weights(): pl.pallas_call(kernel, out_shape=jax.ShapeDtypeStruct((blocks, sources, h...  68.9 us
    ppermute x14, starting transfers between devices, rotated(): lax.ppermute(value, axis, [(k, (k + shift) % size) for k in range(size)])  17.8 us
    ppermute x23, starting transfers between devices, swapped(): return lax.ppermute(value, axis, [(k, k ^ bit) for k in range(size)])  17.2 us
    ppermute x14, waiting for transfers between devices, rotated(): lax.ppermute(value, axis, [(k, (k + shift) % size) for k in range(size)])  16.2 us
    ppermute x1, waiting for transfers between devices, line_gather(): second = jnp.where(inner, middle, lax.ppermute(middle, axis, outward))  8.12 us
  transfers between devices with their start and end apart: 41, of which 14 were waited for; matrix products, arithmetic and copies ran while one was open for 5% of the time, Pallas kernels for 36%

commit v1 on v0

--- a/solution.py
+++ b/solution.py
@@ -13,7 +13,6 @@
 HD = 128
 GROUP = H // KV
 LANES = 128
-FIRST = 256
 
 
 def rotated(value, axis, shift):
@@ -88,7 +87,7 @@
 
 PAD = 8
 UNROLL = 32
-HEADS_TOGETHER = 4
+HEADS_TOGETHER = 8
 STEP = 128
 
 
@@ -113,9 +112,11 @@
     packs = held.shape[1] // key_width
     pack_rows = pieces[0].shape[0] - piece
     share = sources // parts // 2
-    step_at = pl.program_id(0)
-
-    @pl.when(step_at == 0)
+    step_at = pl.num_programs(0) - 1 - pl.program_id(0)
+    half_at = pl.program_id(1)
+    half = sources // 2
+
+    @pl.when((pl.program_id(0) == 0) & (half_at == 0))
     def _():
         for bit, ref in enumerate(pieces[:2]):
             origin = (here_row ^ bit) % 2
@@ -131,7 +132,7 @@
         want = step_at * per + slot
         for bit, ref in enumerate(pieces):
 
-            @pl.when(here_row ^ bit == want)
+            @pl.when((here_row ^ bit == want) & (half_at == 0))
             def _(ref=ref, slot=slot):
                 held[slot * piece : (slot + 1) * piece, :] = ref[:piece, :]
 
@@ -140,7 +141,7 @@
 
     for block, (low, high) in enumerate(limits):
 
-        @pl.when(step_at == block)
+        @pl.when((step_at == block) & (half_at == 0))
         def _(block=block, low=low, high=high):
             local = block * LANES + lax.broadcasted_iota(jnp.int32, (1, LANES), 1)
             row = local // piece
@@ -180,18 +181,21 @@
                 return carry
 
             lax.fori_loop(0, here_heads // together, several, 0)
-            flat = stage.reshape(here_heads * (sources + PAD), LANES)
-            factors = scales[pl.ds(0, here_heads, stride=8), :]
-            each = 16
-
-            def cast(step, carry):
-                for inner in range(each):
-                    at = step * each + inner
-                    value = flat[pl.ds(at, here_heads, stride=sources + PAD), :]
-                    o_ref[at] = (value * factors).astype(jnp.bfloat16)
-                return carry
-
-            lax.fori_loop(0, high // each, cast, 0, unroll=2)
+
+    flat = stage.reshape(here_heads * (sources + PAD), LANES)
+    factors = scales[pl.ds(0, here_heads, stride=8), :]
+    each = 16
+    top = (((step_at + 1) * LANES - 1) // piece + 1) * rows
+    count = jnp.clip(top - half_at * half, 0, half)
+
+    def cast(step, carry):
+        for inner in range(each):
+            at = step * each + inner
+            value = flat[pl.ds(half_at * half + at, here_heads, stride=sources + PAD), :]
+            o_ref[at] = (value * factors).astype(jnp.bfloat16)
+        return carry
+
+    lax.fori_loop(0, count // each, cast, 0)
 
 
 def head_weights(place, pieces, rows, parts, sources, key_width):
@@ -218,19 +222,23 @@
         scale=math.log2(math.e) / math.sqrt(HD),
     )
     work = count * sources * here_heads
+
+    def written(b, j, place):
+        block = blocks - 1 - b
+        top = (((block + 1) * LANES - 1) // piece + 1) * rows
+        return block, jnp.where(top > sources // 2, j, 0), 0, 0
+
     return pl.pallas_call(
         kernel,
         out_shape=jax.ShapeDtypeStruct((blocks, sources, here_heads, LANES), jnp.bfloat16),
         grid_spec=pltpu.PrefetchScalarGridSpec(
             num_scalar_prefetch=1,
-            grid=(blocks,),
+            grid=(blocks, 2),
             in_specs=[
-                pl.BlockSpec(p.shape, lambda b, place: (0, 0), pipeline_mode=pl.Buffered(1))
+                pl.BlockSpec(p.shape, lambda b, j, place: (0, 0), pipeline_mode=pl.Buffered(1))
                 for p in pieces
             ],
-            out_specs=pl.BlockSpec(
-                (None, sources, here_heads, LANES), lambda b, place: (b, 0, 0, 0)
-            ),
+            out_specs=pl.BlockSpec((None, sources // 2, here_heads, LANES), written),
             scratch_shapes=[
                 pltpu.VMEM((here_heads, sources + PAD, LANES), jnp.float32),
                 pltpu.VMEM((here_heads * 8, LANES), jnp.float32),
@@ -246,15 +254,11 @@
     )(place, *pieces)
 
 
-def norms_kernel(place_ref, v_ref, *refs, rows, parts, row_devices, spans, first):
+def norms_kernel(place_ref, v_ref, *refs, rows, parts, row_devices, spans):
     here_src, here_row = place_ref[0], place_ref[1]
     wo_refs = refs[: parts * row_devices]
     w_refs = refs[parts * row_devices : parts * row_devices + spans]
-    rest = refs[parts * row_devices + spans :]
-    if first:
-        o_ref, stage, flipped = rest
-    else:
-        before_ref, o_ref, stage, flipped = rest
+    o_ref, stage, flipped = refs[parts * row_devices + spans :]
     sources = v_ref.shape[0]
     local_rows, cols = wo_refs[0].shape
     span_heads = H // spans
@@ -295,11 +299,12 @@
         def _(begin=begin):
             if begin:
                 flipped[:, :begin] = jnp.zeros((sources, begin), jnp.float32)
+            unroll = UNROLL if begin else UNROLL // 2
 
             def several(step, carry):
                 found = []
-                for inner in range(UNROLL):
-                    col = step * UNROLL + inner
+                for inner in range(unroll):
+                    col = step * unroll + inner
                     attend = jnp.concatenate(
                         [
                             jnp.concatenate([ref[block, col] for ref in w_refs], axis=0)
@@ -327,18 +332,17 @@
                     )
                     found.append(jnp.sum(jnp.abs(contrib), axis=0, keepdims=True))
                     if len(found) == 8:
-                        at = pl.multiple_of(step * UNROLL + inner - 7, 8)
+                        at = pl.multiple_of(step * unroll + inner - 7, 8)
                         flipped[pl.ds(at, 8), begin:] = jnp.concatenate(found, axis=0)
                         found = []
                 return carry
 
-            lax.fori_loop(0, sources // UNROLL, several, 0)
-
-    found = flipped[...].T
-    o_ref[...] = found if first else before_ref[...] + found
-
-
-def partial_norms(place, values, projections, weights, before, rows, parts):
+            lax.fori_loop(0, sources // unroll, several, 0)
+
+    o_ref[...] = flipped[...].T
+
+
+def partial_norms(place, values, projections, weights, rows, parts):
     row_devices = len(projections) // parts
     sources = values.shape[0]
     count = weights[0].shape[0] * LANES
@@ -350,7 +354,6 @@
         parts=parts,
         row_devices=row_devices,
         spans=len(weights),
-        first=before is None,
     )
     in_specs = [pl.BlockSpec((step, values.shape[1]), lambda b, place: (b, 0))]
     in_specs += [
@@ -363,9 +366,6 @@
     ]
     args = [values, *projections, *weights]
     out_spec = pl.BlockSpec((count, step), lambda b, place: (0, b))
-    if before is not None:
-        in_specs.append(out_spec)
-        args.append(before)
     return pl.pallas_call(
         kernel,
         out_shape=jax.ShapeDtypeStruct((count, sources), jnp.float32),
@@ -419,19 +419,13 @@
 
     _, cols = out_proj.shape
     each = cols // row_devices
-    sizes = [FIRST, each - FIRST] if each > FIRST and each % LANES == 0 else [each]
-    norms = None
-    begin = 0
-    for size in sizes:
-        projections = []
-        for bit in range(row_devices):
-            at = (here_row ^ bit) * each + begin
-            block = lax.dynamic_slice_in_dim(out_proj, at, size, 1)
-            if bit:
-                block = swapped(block, "row", bit)
-            projections += gathered(block, "src")
-        norms = partial_norms(place, values, projections, weights, norms, rows, parts)
-        begin += size
+    projections = []
+    for bit in range(row_devices):
+        block = lax.dynamic_slice_in_dim(out_proj, (here_row ^ bit) * each, each, 1)
+        if bit:
+            block = swapped(block, "row", bit)
+        projections += gathered(block, "src")
+    norms = partial_norms(place, values, projections, weights, rows, parts)
 
     stacked = norms.reshape(row_devices, piece, sources)
     held = [

time: 368 us -> 367 us (level)
  waiting for transfers between devices: 97.4 us -> 121 us
  Pallas kernels: 199 us -> 184 us
  local copies, waits for them, and re-layouts: 21.5 us -> 17.6 us
    ppermute x23 -> x20, waiting for transfers between devices: 71.3 us -> 99.9 us  [swapped(): return lax.ppermute(value, axis, [(k, k ^ bit) for k in range(size)])]
    pallas_call x2 -> x1, Pallas kernels: 130 us -> 115 us  [partial_norms(): pl.pallas_call(kernel, out_shape=jax.ShapeDtypeStruct((count, sources), j...]
    ppermute x1, waiting for transfers between devices: 8.12 us -> 1.59 us  [line_gather(): second = jnp.where(inner, middle, lax.ppermute(middle, axis, outward))]
    ppermute x14 -> x10, waiting for transfers between devices: 16.2 us -> 19.6 us  [rotated(): lax.ppermute(value, axis, [(k, (k + shift) % size) for k in range(size)])]
    ppermute x23 -> x20, starting transfers between devices: 17.2 us -> 14.2 us  [swapped(): return lax.ppermute(value, axis, [(k, k ^ bit) for k in range(size)])]
    ppermute x14 -> x10, starting transfers between devices: 17.8 us -> 17.4 us  [rotated(): lax.ppermute(value, axis, [(k, (k + shift) % size) for k in range(size)])]
  transfers between devices with their start and end apart: 41 -> 34, of which waited for: 14 -> 17; matrix products, arithmetic and copies ran while one was open for 5% -> 4% of each run, Pallas kernels for 36% -> 19%
where the time goes in v1:
time: 367 us; the launch traced here: 366 us
  Pallas kernels  184 us (50%)
  waiting for transfers between devices  121 us (33%)
  starting transfers between devices  37.3 us (10%)
  local copies, waits for them, and re-layouts  17.6 us (5%)
  other arithmetic  5.65 us (2%)
    pallas_call x1, Pallas kernels, partial_norms(): pl.pallas_call(kernel, out_shape=jax.ShapeDtypeStruct((count, sources), j...  115 us
    ppermute x20, waiting for transfers between devices, swapped(): return lax.ppermute(value, axis, [(k, k ^ bit) for k in range(size)])  99.9 us
    pallas_call x4, Pallas kernels, head_weights(): pl.pallas_call(kernel, out_shape=jax.ShapeDtypeStruct((blocks, sources, h...  68.9 us
    ppermute x10, waiting for transfers between devices, rotated(): lax.ppermute(value, axis, [(k, (k + shift) % size) for k in range(size)])  19.6 us
    ppermute x10, starting transfers between devices, rotated(): lax.ppermute(value, axis, [(k, (k + shift) % size) for k in range(size)])  17.4 us
    ppermute x20, starting transfers between devices, swapped(): return lax.ppermute(value, axis, [(k, k ^ bit) for k in range(size)])  14.2 us
  transfers between devices with their start and end apart: 34, of which 17 were waited for; matrix products, arithmetic and copies ran while one was open for 4% of the time, Pallas kernels for 19%

profile of v1, /device:TPU:0, one launch (start us, length us, event | category | flops | bytes accessed | tf_op | source)
XLA Modules:
  0.0 366.4 jit_solution(4510566503017568657)
XLA Ops:
  1.0 3.0 collective-permute-start.9
  4.0 1.9 constant_dynamic-slice_fusion.11
  8.9 1.6 collective-permute-start.17
  10.5 3.8 %collective-permute-start.13 = (bf16[192,2048]{1,0:T(8,128)(2,1)S(1)}, bf16[192,2048]{1,0:T(8,128)(2,1)S(1)}, u32[]{:S(2)}, u32[]{:S(2)}) collective-permute-start(bf16[192,2048]{1,0:T(8,128)(2,1)S(1)} %pad_maximum_fusion.1.refs_0_), channel_id=1, source_target_pairs={{0,8},{8,0},{16,24},{24,16},{1,9},{9,1},{17,25},{25,17},{2,10},{10... | collective-permute-start | bytes 2359304 | tf_op jit(solution)/shard_map/ppermute | solution.py:37
  15.5 15.1 %collective-permute-done.13.refs_0_ = bf16[192,2048]{1,0:T(8,128)(2,1)S(1)} collective-permute-done((bf16[192,2048]{1,0:T(8,128)(2,1)S(1)}, bf16[192,2048]{1,0:T(8,128)(2,1)S(1)}, u32[]{:S(2)}, u32[]{:S(2)}) %collective-permute-start.13) | collective-permute-done | bytes 786464 | tf_op jit(solution)/shard_map/ppermute | solution.py:37
  30.7 1.5 collective-permute-start.22
  36.0 3.5 constant_dynamic-slice_fusion.12
  39.5 5.0 %collective-permute-done.11.refs_2_ = bf16[128,2048]{1,0:T(8,128)(2,1)} collective-permute-done((bf16[128,2048]{1,0:T(8,128)(2,1)}, bf16[128,2048]{1,0:T(8,128)(2,1)}, u32[]{:S(2)}, u32[]{:S(2)}) %collective-permute-start.11) | collective-permute-done | bytes 524320 | tf_op jit(solution)/shard_map/ppermute | solution.py:37
  44.5 2.0 collective-permute-done
  46.9 1.6 collective-permute-done.18
  48.5 1.6 collective-permute-start.12
  54.2 18.4 %collective-permute-done.5.refs_4_ = bf16[1024,512]{1,0:T(8,128)(2,1)} collective-permute-done((bf16[1024,512]{1,0:T(8,128)(2,1)S(1)}, bf16[1024,512]{1,0:T(8,128)(2,1)}, u32[]{:S(2)}, u32[]{:S(2)}) %collective-permute-start.5) | collective-permute-done | bytes 1048608 | tf_op jit(solution)/shard_map/ppermute | solution.py:37
  73.1 19.8 %collective-permute-done.7.refs_6_ = bf16[1024,512]{1,0:T(8,128)(2,1)} collective-permute-done((bf16[1024,512]{1,0:T(8,128)(2,1)S(1)}, bf16[1024,512]{1,0:T(8,128)(2,1)}, u32[]{:S(2)}, u32[]{:S(2)}) %collective-permute-start.7) | collective-permute-done | bytes 1048608 | tf_op jit(solution)/shard_map/ppermute | solution.py:37
  93.0 1.9 collective-permute-start.19
  95.5 10.7 %collective-permute-done.15.refs_2_ = bf16[128,2048]{1,0:T(8,128)(2,1)S(1)} collective-permute-done((bf16[128,2048]{1,0:T(8,128)(2,1)S(1)}, bf16[128,2048]{1,0:T(8,128)(2,1)S(1)}, u32[]{:S(2)}, u32[]{:S(2)}) %collective-permute-start.15) | collective-permute-done | bytes 524320 | tf_op jit(solution)/shard_map/ppermute | solution.py:37
  106.7 8.3 %collective-permute-done.20.refs_2_ = bf16[128,2048]{1,0:T(8,128)(2,1)S(1)} collective-permute-done((bf16[128,2048]{1,0:T(8,128)(2,1)S(1)}, bf16[128,2048]{1,0:T(8,128)(2,1)S(1)}, u32[]{:S(2)}, u32[]{:S(2)}) %collective-permute-start.20) | collective-permute-done | bytes 524320 | tf_op jit(solution)/shard_map/ppermute | solution.py:37
  115.0 1.6 collective-permute-start.25
  120.3 9.2 %collective-permute-done.25.refs_2_ = bf16[128,2048]{1,0:T(8,128)(2,1)} collective-permute-done((bf16[128,2048]{1,0:T(8,128)(2,1)S(1)}, bf16[128,2048]{1,0:T(8,128)(2,1)}, u32[]{:S(2)}, u32[]{:S(2)}) %collective-permute-start.25) | collective-permute-done | bytes 524320 | tf_op jit(solution)/shard_map/ppermute | solution.py:37
  129.4 1.6 collective-permute-start.8
  132.3 1.9 stack.49.place_ref
  134.1 17.3 %head_weights.4.refs_8_ = bf16[4,1024,16,128]{3,2,1,0:T(8,128)(2,1)} custom-call(s32[6]{0:T(128)} %stack.49.place_ref, bf16[192,2048]{1,0:T(8,128)(2,1)} %copy-done.4, bf16[192,2048]{1,0:T(8,128)(2,1)} %collective-permute-done.10.refs_1_, bf16[128,2048]{1,0:T(8,128)(2,1)} %collective-permute-done.11.refs_2_, bf16[128,2048]{1,0:T(8,128)(2,1)} %copy-done.10), custom_call_target="tpu_custom_call" | custom-call | flops 1073741824 | bytes 16777216 | tf_op jit(solution)/shard_map/head_weights/pallas_call | solution.py:231
  154.1 17.1 %head_weights.5.refs_9_ = bf16[4,1024,16,128]{3,2,1,0:T(8,128)(2,1)} custom-call(s32[6]{0:T(128)} %stack.49.place_ref, bf16[192,2048]{1,0:T(8,128)(2,1)} %copy-done.5, bf16[192,2048]{1,0:T(8,128)(2,1)} %copy-done.8, bf16[128,2048]{1,0:T(8,128)(2,1)} %copy-done.11, bf16[128,2048]{1,0:T(8,128)(2,1)} %copy-done.13), custom_call_target="tpu_custom_call" | custom-call | flops 1073741824 | bytes 16777216 | tf_op jit(solution)/shard_map/head_weights/pallas_call | solution.py:231
  171.2 17.4 %head_weights.6.refs_10_ = bf16[4,1024,16,128]{3,2,1,0:T(8,128)(2,1)} custom-call(s32[6]{0:T(128)} %stack.49.place_ref, bf16[192,2048]{1,0:T(8,128)(2,1)} %copy-done.2, bf16[192,2048]{1,0:T(8,128)(2,1)} %copy-done.9, bf16[128,2048]{1,0:T(8,128)(2,1)} %copy-done.12, bf16[128,2048]{1,0:T(8,128)(2,1)} %copy-done.14), custom_call_target="tpu_custom_call" | custom-call | flops 1073741824 | bytes 16777216 | tf_op jit(solution)/shard_map/head_weights/pallas_call | solution.py:231
  188.6 17.2 %head_weights.7.refs_11_ = bf16[4,1024,16,128]{3,2,1,0:T(8,128)(2,1)} custom-call(s32[6]{0:T(128)} %stack.49.place_ref, bf16[192,2048]{1,0:T(8,128)(2,1)} %copy-done.3, bf16[192,2048]{1,0:T(8,128)(2,1)} %collective-permute-done.24.refs_1_, bf16[128,2048]{1,0:T(8,128)(2,1)} %collective-permute-done.25.refs_2_, bf16[128,2048]{1,0:T(8,128)(2,1)} %collective-permute-done.26.refs_3_), custom_call_target="tpu_custom_call" | custom-call | flops 1073741824 | bytes 16777216 | tf_op jit(solution)/shard_map/head_weights/pallas_call | solution.py:231
  205.8 3.8 %collective-permute-done.8.refs_7_ = bf16[1024,512]{1,0:T(8,128)(2,1)} collective-permute-done((bf16[1024,512]{1,0:T(8,128)(2,1)}, bf16[1024,512]{1,0:T(8,128)(2,1)}, u32[]{:S(2)}, u32[]{:S(2)}) %collective-permute-start.8) | collective-permute-done | bytes 1048608 | tf_op jit(solution)/shard_map/ppermute | solution.py:20
  209.5 115.4 %partial_norms.1 = f32[512,1024]{1,0:T(8,128)} custom-call(s32[6]{0:T(128)} %stack.49.place_ref, bf16[1024,1024]{1,0:T(8,128)(2,1)} %bitcast.47, bf16[1024,512]{1,0:T(8,128)(2,1)} %get-tuple-element.11.refs_0_, bf16[1024,512]{1,0:T(8,128)(2,1)} %collective-permute-done.2.refs_1_, bf16[1024,512]{1,0:T(8,128)(2,1)} %collective-permute-done.3.refs_2_, ...), custom_call_target="tpu_custom_call" | custom-call | flops 25769803776 | bytes 67108864 | tf_op jit(solution)/shard_map/partial_norms/pallas_call | solution.py:369
  325.0 1.7 constant_dynamic-slice_fusion.9
  330.4 12.5 %collective-permute-done.29 = f32[128,1024]{0,1:T(8,128)S(1)} collective-permute-done((f32[128,1024]{0,1:T(8,128)S(1)}, f32[128,1024]{0,1:T(8,128)S(1)}, u32[]{:S(2)}, u32[]{:S(2)}) %collective-permute-start.29) | collective-permute-done | bytes 524320 | tf_op jit(solution)/shard_map/ppermute | solution.py:37
  344.1 7.2 %collective-permute-done.30 = f32[129,512]{1,0:T(8,128)S(1)} collective-permute-done((f32[129,512]{1,0:T(8,128)S(1)}, f32[129,512]{1,0:T(8,128)S(1)}, u32[]{:S(2)}, u32[]{:S(2)}) %collective-permute-start.30) | collective-permute-done | bytes 264224 | tf_op jit(solution)/shard_map/ppermute | solution.py:20
  352.3 4.5 %collective-permute-start.31 = (f32[258,128]{1,0:T(8,128)S(1)}, f32[258,128]{1,0:T(8,128)S(1)}, u32[]{:S(2)}, u32[]{:S(2)}) collective-permute-start(f32[258,128]{1,0:T(8,128)S(1)} %get-tuple-element.27), channel_id=1, source_target_pairs={{0,8},{8,16},{16,24},{24,0},{1,9},{9,17},{17,25},{25,1},{2,10},{10... | collective-permute-start | bytes 396296 | tf_op jit(solution)/shard_map/ppermute | solution.py:20
  356.8 2.8 collective-permute-start.33
  360.8 4.8 %collective-permute-done.32 = f32[258,128]{1,0:T(8,128)S(1)} collective-permute-done((f32[258,128]{1,0:T(8,128)S(1)}, f32[258,128]{1,0:T(8,128)S(1)}, u32[]{:S(2)}, u32[]{:S(2)}) %collective-permute-start.32) | collective-permute-done | bytes 132128 | tf_op jit(solution)/shard_map/ppermute | solution.py:20
  (119 shorter events, 30.5 us)
Async XLA Ops:
  1.0 6.5 %collective-permute-start.9 = (bf16[256,256]{1,0:T(8,128)(2,1)S(1)}, bf16[256,256]{1,0:T(8,128)(2,1)S(1)}, u32[]{:S(2)}, u32[]{:S(2)}) collective-permute-start(bf16[256,256]{1,0:T(8,128)(2,1)S(1)} %constant_dynamic-slice_fusion.10), channel_id=1, source_target_pairs={{0,1},{1,0},{2,3},{3,2},{4,5},{5,4},{6,7},{7,6},{8,9},{9,8},{10,11... | collective-permute-start | bytes 393224 | tf_op jit(solution)/shard_map/ppermute | solution.py:20
  8.9 5.4 %collective-permute-start.17 = (bf16[192,2048]{1,0:T(8,128)(2,1)S(1)}, bf16[192,2048]{1,0:T(8,128)(2,1)}, u32[]{:S(2)}, u32[]{:S(2)}) collective-permute-start(bf16[192,2048]{1,0:T(8,128)(2,1)S(1)} %pad_maximum_fusion.1.refs_0_), channel_id=1, source_target_pairs={{8,16},{16,8},{9,17},{17,9},{10,18},{18,10},{11,19},{19,11},{12,20... | collective-permute-start | bytes 2359304 | tf_op jit(solution)/shard_map/ppermute | solution.py:75
  10.5 20.2 %collective-permute-start.13 = (bf16[192,2048]{1,0:T(8,128)(2,1)S(1)}, bf16[192,2048]{1,0:T(8,128)(2,1)S(1)}, u32[]{:S(2)}, u32[]{:S(2)}) collective-permute-start(bf16[192,2048]{1,0:T(8,128)(2,1)S(1)} %pad_maximum_fusion.1.refs_0_), channel_id=1, source_target_pairs={{0,8},{8,0},{16,24},{24,16},{1,9},{9,1},{17,25},{25,17},{2,10},{10... | collective-permute-start | bytes 2359304 | tf_op jit(solution)/shard_map/ppermute | solution.py:37
  14.3 34.3 %collective-permute-start.18 = (bf16[192,2048]{1,0:T(8,128)(2,1)}, bf16[192,2048]{1,0:T(8,128)(2,1)}, u32[]{:S(2)}, u32[]{:S(2)}) collective-permute-start(bf16[192,2048]{1,0:T(8,128)(2,1)} %collective-permute-done.17), channel_id=1, source_target_pairs={{8,0},{16,24},{9,1},{17,25},{10,2},{18,26},{11,3},{19,27},{12,4},{... | collective-permute-start | bytes 2359304 | tf_op jit(solution)/shard_map/ppermute | solution.py:77
  30.7 17.9 %collective-permute-start.22 = (bf16[192,2048]{1,0:T(8,128)(2,1)S(1)}, bf16[192,2048]{1,0:T(8,128)(2,1)}, u32[]{:S(2)}, u32[]{:S(2)}) collective-permute-start(bf16[192,2048]{1,0:T(8,128)(2,1)S(1)} %collective-permute-done.13.refs_0_), channel_id=1, source_target_pairs={{8,16},{16,8},{9,17},{17,9},{10,18},{18,10},{11,19},{19,11},{12,20... | collective-permute-start | bytes 2359304 | tf_op jit(solution)/shard_map/ppermute | solution.py:76
  32.2 12.3 %collective-permute-start.11 = (bf16[128,2048]{1,0:T(8,128)(2,1)}, bf16[128,2048]{1,0:T(8,128)(2,1)}, u32[]{:S(2)}, u32[]{:S(2)}) collective-permute-start(bf16[128,2048]{1,0:T(8,128)(2,1)} %constant_dynamic-slice_fusion.11), channel_id=1, source_target_pairs={{0,4},{2,6},{4,0},{6,2},{1,5},{3,7},{5,1},{7,3},{8,12},{10,14},{12... | collective-permute-start | bytes 1572872 | tf_op jit(solution)/shard_map/ppermute | solution.py:37
  34.5 11.9 %collective-permute-start = (bf16[256,1024]{1,0:T(8,128)(2,1)}, bf16[256,1024]{1,0:T(8,128)(2,1)S(1)}, u32[]{:S(2)}, u32[]{:S(2)}) collective-permute-start(bf16[256,1024]{1,0:T(8,128)(2,1)} %constant_dynamic-slice_fusion.16), channel_id=1, source_target_pairs={{0,1},{1,0},{2,3},{3,2},{4,5},{5,4},{6,7},{7,6},{8,9},{9,8},{10,11... | collective-permute-start | bytes 1572872 | tf_op jit(solution)/shard_map/ppermute | solution.py:20
  36.0 15.4 %collective-permute-start.10 = (bf16[192,2048]{1,0:T(8,128)(2,1)S(1)}, bf16[192,2048]{1,0:T(8,128)(2,1)}, u32[]{:S(2)}, u32[]{:S(2)}) collective-permute-start(bf16[192,2048]{1,0:T(8,128)(2,1)S(1)} %pad_maximum_fusion.1.refs_0_), channel_id=1, source_target_pairs={{0,2},{2,0},{4,6},{6,4},{1,3},{3,1},{5,7},{7,5},{8,10},{10,8},{12,... | collective-permute-start | bytes 2359304 | tf_op jit(solution)/shard_map/ppermute | solution.py:37
  44.5 9.1 %collective-permute-start.3 = (bf16[1024,512]{1,0:T(8,128)(2,1)S(1)}, bf16[1024,512]{1,0:T(8,128)(2,1)}, u32[]{:S(2)}, u32[]{:S(2)}) collective-permute-start(bf16[1024,512]{1,0:T(8,128)(2,1)S(1)} %get-tuple-element.10), channel_id=1, source_target_pairs={{0,2},{2,0},{4,6},{6,4},{1,3},{3,1},{5,7},{7,5},{8,10},{10,8},{12,... | collective-permute-start | bytes 3145736 | tf_op jit(solution)/shard_map/ppermute | solution.py:37
  46.4 26.1 %collective-permute-start.5 = (bf16[1024,512]{1,0:T(8,128)(2,1)S(1)}, bf16[1024,512]{1,0:T(8,128)(2,1)}, u32[]{:S(2)}, u32[]{:S(2)}) collective-permute-start(bf16[1024,512]{1,0:T(8,128)(2,1)S(1)} %get-tuple-element.12), channel_id=1, source_target_pairs={{0,4},{2,6},{4,0},{6,2},{1,5},{3,7},{5,1},{7,3},{8,12},{10,14},{12... | collective-permute-start | bytes 3145736 | tf_op jit(solution)/shard_map/ppermute | solution.py:37
  48.5 44.4 %collective-permute-start.7 = (bf16[1024,512]{1,0:T(8,128)(2,1)S(1)}, bf16[1024,512]{1,0:T(8,128)(2,1)}, u32[]{:S(2)}, u32[]{:S(2)}) collective-permute-start(bf16[1024,512]{1,0:T(8,128)(2,1)S(1)} %get-tuple-element.9), channel_id=1, source_target_pairs={{0,6},{2,4},{4,2},{6,0},{1,7},{3,5},{5,3},{7,1},{8,14},{10,12},{12... | collective-permute-start | bytes 3145736 | tf_op jit(solution)/shard_map/ppermute | solution.py:37
  48.5 5.0 %collective-permute-start.12 = (bf16[128,2048]{1,0:T(8,128)(2,1)}, bf16[128,2048]{1,0:T(8,128)(2,1)S(1)}, u32[]{:S(2)}, u32[]{:S(2)}) collective-permute-start(bf16[128,2048]{1,0:T(8,128)(2,1)} %collective-permute-done.11.refs_2_), channel_id=1, source_target_pairs={{0,2},{2,0},{4,6},{6,4},{1,3},{3,1},{5,7},{7,5},{8,10},{10,8},{12,... | collective-permute-start | bytes 1572872 | tf_op jit(solution)/shard_map/ppermute | solution.py:37
  51.4 43.5 %collective-permute-start.23 = (bf16[192,2048]{1,0:T(8,128)(2,1)}, bf16[192,2048]{1,0:T(8,128)(2,1)S(1)}, u32[]{:S(2)}, u32[]{:S(2)}) collective-permute-start(bf16[192,2048]{1,0:T(8,128)(2,1)} %collective-permute-done.22), channel_id=1, source_target_pairs={{8,0},{16,24},{9,1},{17,25},{10,2},{18,26},{11,3},{19,27},{12,4},{... | collective-permute-start | bytes 2359304 | tf_op jit(solution)/shard_map/ppermute | solution.py:78
  53.5 52.7 %collective-permute-start.1 = (bf16[2,256,1024]{2,1,0:T(8,128)(2,1)S(1)}, bf16[2,256,1024]{2,1,0:T(8,128)(2,1)S(1)}, u32[]{:S(2)}, u32[]{:S(2)}) collective-permute-start(bf16[2,256,1024]{2,1,0:T(8,128)(2,1)S(1)} %fusion.2), channel_id=1, source_target_pairs={{0,2},{2,0},{4,6},{6,4},{1,3},{3,1},{5,7},{7,5},{8,10},{10,8},{12,... | collective-permute-start | bytes 3145736 | tf_op jit(solution)/shard_map/ppermute | solution.py:37
  53.6 61.4 %collective-permute-start.14 = (bf16[192,2048]{1,0:T(8,128)(2,1)S(1)}, bf16[192,2048]{1,0:T(8,128)(2,1)S(1)}, u32[]{:S(2)}, u32[]{:S(2)}) collective-permute-start(bf16[192,2048]{1,0:T(8,128)(2,1)S(1)} %collective-permute-done.13.refs_0_), channel_id=1, source_target_pairs={{0,2},{2,0},{4,6},{6,4},{1,3},{3,1},{5,7},{7,5},{8,10},{10,8},{12,... | collective-permute-start | bytes 2359304 | tf_op jit(solution)/shard_map/ppermute | solution.py:37
  72.6 33.6 %collective-permute-start.15 = (bf16[128,2048]{1,0:T(8,128)(2,1)S(1)}, bf16[128,2048]{1,0:T(8,128)(2,1)S(1)}, u32[]{:S(2)}, u32[]{:S(2)}) collective-permute-start(bf16[128,2048]{1,0:T(8,128)(2,1)S(1)} %slice.28), channel_id=1, source_target_pairs={{0,4},{2,6},{4,0},{6,2},{1,5},{3,7},{5,1},{7,3},{8,12},{10,14},{12... | collective-permute-start | bytes 1572872 | tf_op jit(solution)/shard_map/ppermute | solution.py:37
  93.0 25.1 %collective-permute-start.19 = (bf16[192,2048]{1,0:T(8,128)(2,1)S(1)}, bf16[192,2048]{1,0:T(8,128)(2,1)S(1)}, u32[]{:S(2)}, u32[]{:S(2)}) collective-permute-start(bf16[192,2048]{1,0:T(8,128)(2,1)S(1)} %broadcast_select_fusion.1.refs_0_), channel_id=1, source_target_pairs={{0,2},{2,0},{4,6},{6,4},{1,3},{3,1},{5,7},{7,5},{8,10},{10,8},{12,... | collective-permute-start | bytes 2359304 | tf_op jit(solution)/shard_map/ppermute | solution.py:37
  94.9 20.1 %collective-permute-start.20 = (bf16[128,2048]{1,0:T(8,128)(2,1)S(1)}, bf16[128,2048]{1,0:T(8,128)(2,1)S(1)}, u32[]{:S(2)}, u32[]{:S(2)}) collective-permute-start(bf16[128,2048]{1,0:T(8,128)(2,1)S(1)} %slice.29), channel_id=1, source_target_pairs={{0,4},{2,6},{4,0},{6,2},{1,5},{3,7},{5,1},{7,3},{8,12},{10,14},{12... | collective-permute-start | bytes 1572872 | tf_op jit(solution)/shard_map/ppermute | solution.py:37
  106.2 45.2 %collective-permute-start.24 = (bf16[192,2048]{1,0:T(8,128)(2,1)S(1)}, bf16[192,2048]{1,0:T(8,128)(2,1)}, u32[]{:S(2)}, u32[]{:S(2)}) collective-permute-start(bf16[192,2048]{1,0:T(8,128)(2,1)S(1)} %broadcast_select_fusion.refs_0_), channel_id=1, source_target_pairs={{0,2},{2,0},{4,6},{6,4},{1,3},{3,1},{5,7},{7,5},{8,10},{10,8},{12,... | collective-permute-start | bytes 2359304 | tf_op jit(solution)/shard_map/ppermute | solution.py:37
  106.2 10.4 %collective-permute-start.16 = (bf16[128,2048]{1,0:T(8,128)(2,1)S(1)}, bf16[128,2048]{1,0:T(8,128)(2,1)S(1)}, u32[]{:S(2)}, u32[]{:S(2)}) collective-permute-start(bf16[128,2048]{1,0:T(8,128)(2,1)S(1)} %collective-permute-done.15.refs_2_), channel_id=1, source_target_pairs={{0,2},{2,0},{4,6},{6,4},{1,3},{3,1},{5,7},{7,5},{8,10},{10,8},{12,... | collective-permute-start | bytes 1572872 | tf_op jit(solution)/shard_map/ppermute | solution.py:37
  115.0 3.7 %collective-permute-start.21 = (bf16[128,2048]{1,0:T(8,128)(2,1)S(1)}, bf16[128,2048]{1,0:T(8,128)(2,1)S(1)}, u32[]{:S(2)}, u32[]{:S(2)}) collective-permute-start(bf16[128,2048]{1,0:T(8,128)(2,1)S(1)} %collective-permute-done.20.refs_2_), channel_id=1, source_target_pairs={{0,2},{2,0},{4,6},{6,4},{1,3},{3,1},{5,7},{7,5},{8,10},{10,8},{12,... | collective-permute-start | bytes 1572872 | tf_op jit(solution)/shard_map/ppermute | solution.py:37
  115.0 14.4 %collective-permute-start.25 = (bf16[128,2048]{1,0:T(8,128)(2,1)S(1)}, bf16[128,2048]{1,0:T(8,128)(2,1)}, u32[]{:S(2)}, u32[]{:S(2)}) collective-permute-start(bf16[128,2048]{1,0:T(8,128)(2,1)S(1)} %slice.30), channel_id=1, source_target_pairs={{0,4},{2,6},{4,0},{6,2},{1,5},{3,7},{5,1},{7,3},{8,12},{10,14},{12... | collective-permute-start | bytes 1572872 | tf_op jit(solution)/shard_map/ppermute | solution.py:37
  116.6 89.1 %collective-permute-start.2 = (bf16[1024,512]{1,0:T(8,128)(2,1)}, bf16[1024,512]{1,0:T(8,128)(2,1)}, u32[]{:S(2)}, u32[]{:S(2)}) collective-permute-start(bf16[1024,512]{1,0:T(8,128)(2,1)} %get-tuple-element.11.refs_0_), channel_id=1, source_target_pairs={{0,1},{1,0},{2,3},{3,2},{4,5},{5,4},{6,7},{7,6},{8,9},{9,8},{10,11... | collective-permute-start | bytes 3145736 | tf_op jit(solution)/shard_map/ppermute | solution.py:20
  118.1 87.7 %collective-permute-start.4 = (bf16[1024,512]{1,0:T(8,128)(2,1)}, bf16[1024,512]{1,0:T(8,128)(2,1)}, u32[]{:S(2)}, u32[]{:S(2)}) collective-permute-start(bf16[1024,512]{1,0:T(8,128)(2,1)} %collective-permute-done.3.refs_2_), channel_id=1, source_target_pairs={{0,1},{1,0},{2,3},{3,2},{4,5},{5,4},{6,7},{7,6},{8,9},{9,8},{10,11... | collective-permute-start | bytes 3145736 | tf_op jit(solution)/shard_map/ppermute | solution.py:20
  119.0 86.8 %collective-permute-start.6 = (bf16[1024,512]{1,0:T(8,128)(2,1)}, bf16[1024,512]{1,0:T(8,128)(2,1)}, u32[]{:S(2)}, u32[]{:S(2)}) collective-permute-start(bf16[1024,512]{1,0:T(8,128)(2,1)} %collective-permute-done.5.refs_4_), channel_id=1, source_target_pairs={{0,1},{1,0},{2,3},{3,2},{4,5},{5,4},{6,7},{7,6},{8,9},{9,8},{10,11... | collective-permute-start | bytes 3145736 | tf_op jit(solution)/shard_map/ppermute | solution.py:20
  129.4 80.1 %collective-permute-start.8 = (bf16[1024,512]{1,0:T(8,128)(2,1)}, bf16[1024,512]{1,0:T(8,128)(2,1)}, u32[]{:S(2)}, u32[]{:S(2)}) collective-permute-start(bf16[1024,512]{1,0:T(8,128)(2,1)} %collective-permute-done.7.refs_6_), channel_id=1, source_target_pairs={{0,1},{1,0},{2,3},{3,2},{4,5},{5,4},{6,7},{7,6},{8,9},{9,8},{10,11... | collective-permute-start | bytes 3145736 | tf_op jit(solution)/shard_map/ppermute | solution.py:20
  151.4 37.1 %collective-permute-start.26 = (bf16[128,2048]{1,0:T(8,128)(2,1)}, bf16[128,2048]{1,0:T(8,128)(2,1)}, u32[]{:S(2)}, u32[]{:S(2)}) collective-permute-start(bf16[128,2048]{1,0:T(8,128)(2,1)} %collective-permute-done.25.refs_2_), channel_id=1, source_target_pairs={{0,2},{2,0},{4,6},{6,4},{1,3},{3,1},{5,7},{7,5},{8,10},{10,8},{12,... | collective-permute-start | bytes 1572872 | tf_op jit(solution)/shard_map/ppermute | solution.py:37
  328.9 14.0 %collective-permute-start.29 = (f32[128,1024]{0,1:T(8,128)S(1)}, f32[128,1024]{0,1:T(8,128)S(1)}, u32[]{:S(2)}, u32[]{:S(2)}) collective-permute-start(f32[128,1024]{0,1:T(8,128)S(1)} %bitcast_add_fusion), channel_id=1, source_target_pairs={{0,4},{2,6},{4,0},{6,2},{1,5},{3,7},{5,1},{7,3},{8,12},{10,14},{12... | collective-permute-start | bytes 1572872 | tf_op jit(solution)/shard_map/ppermute | solution.py:37
  343.5 7.9 %collective-permute-start.30 = (f32[129,512]{1,0:T(8,128)S(1)}, f32[129,512]{1,0:T(8,128)S(1)}, u32[]{:S(2)}, u32[]{:S(2)}) collective-permute-start(f32[129,512]{1,0:T(8,128)S(1)} %get-tuple-element.26), channel_id=1, source_target_pairs={{0,1},{1,0},{2,3},{3,2},{4,5},{5,4},{6,7},{7,6},{8,9},{9,8},{10,11... | collective-permute-start | bytes 792584 | tf_op jit(solution)/shard_map/ppermute | solution.py:20
  352.3 8.4 %collective-permute-start.31 = (f32[258,128]{1,0:T(8,128)S(1)}, f32[258,128]{1,0:T(8,128)S(1)}, u32[]{:S(2)}, u32[]{:S(2)}) collective-permute-start(f32[258,128]{1,0:T(8,128)S(1)} %get-tuple-element.27), channel_id=1, source_target_pairs={{0,8},{8,16},{16,24},{24,0},{1,9},{9,17},{17,25},{25,1},{2,10},{10... | collective-permute-start | bytes 396296 | tf_op jit(solution)/shard_map/ppermute | solution.py:20
  356.8 8.7 %collective-permute-start.32 = (f32[258,128]{1,0:T(8,128)S(1)}, f32[258,128]{1,0:T(8,128)S(1)}, u32[]{:S(2)}, u32[]{:S(2)}) collective-permute-start(f32[258,128]{1,0:T(8,128)S(1)} %get-tuple-element.28), channel_id=1, source_target_pairs={{0,16},{8,24},{16,0},{24,8},{1,17},{9,25},{17,1},{25,9},{2,18},{10... | collective-permute-start | bytes 396296 | tf_op jit(solution)/shard_map/ppermute | solution.py:20
  356.8 8.7 %collective-permute-start.33 = (f32[258,128]{1,0:T(8,128)S(1)}, f32[258,128]{1,0:T(8,128)S(1)}, u32[]{:S(2)}, u32[]{:S(2)}) collective-permute-start(f32[258,128]{1,0:T(8,128)S(1)} %get-tuple-element.29), channel_id=1, source_target_pairs={{0,24},{8,0},{16,8},{24,16},{1,25},{9,1},{17,9},{25,17},{2,26},{10... | collective-permute-start | bytes 396296 | tf_op jit(solution)/shard_map/ppermute | solution.py:20
  (19 other events, 486.4 us)
